TPU v7x, 32 devices: a whole 2x2x4 slice. The times are simulated.
32 devices in a mesh: dp: 8 (over y, x, core), fsdp: 4 (over z).
Axes of the slice: x: 2, y: 2, z: 4, core: 2. Of those that a mesh axis runs over, the one named last changes fastest.
Arguments:
- patches: bfloat16 [16384, 1024], P(('dp', 'fsdp')), may hold values from -6 to 6
- cotangent: bfloat16 [16384, 1024], P(('dp', 'fsdp')), may hold values from -6 to 6
- ln1_gain: bfloat16 [1024], P('fsdp'), may hold values from 0.5 to 1.5
- ln1_bias: bfloat16 [1024], P('fsdp'), may hold values from -1.75 to 1.75
- w_qkv: bfloat16 [1024, 3072], P('fsdp'), may hold values from -0.1875 to 0.1875
- w_out: bfloat16 [1024, 1024], P('fsdp'), may hold values from -0.5 to 0.5
- ln2_gain: bfloat16 [1024], P('fsdp'), may hold values from 0.5 to 1.5
- ln2_bias: bfloat16 [1024], P('fsdp'), may hold values from -1.75 to 1.75
- w_fc1: bfloat16 [1024, 4096], P('fsdp'), may hold values from -0.1875 to 0.1875
- fc1_bias: bfloat16 [4096], P('fsdp'), may hold values from -3 to 3
- w_fc2: bfloat16 [4096, 1024], P('fsdp'), may hold values from -0.09375 to 0.09375
- pos_table: bfloat16 [50, 1024], P(None, 'fsdp'), may hold values from -3 to 3
- pos_index: int32 [145, 4], replicated, may hold values from 0 to 49, as said below
- pos_weight: float32 [145, 4], replicated, may hold values from 0.1 to 0.6
Outputs:
- block_out: bfloat16 [16384, 1024], P(('dp', 'fsdp'))
- input_grad: bfloat16 [16384, 1024], P(('dp', 'fsdp'))
- ln1_gain_grad: float32 [1024], P('fsdp')
- ln1_bias_grad: float32 [1024], P('fsdp')
- qkv_grad: float32 [1024, 3072], P('fsdp')
- out_proj_grad: float32 [1024, 1024], P('fsdp')
- ln2_gain_grad: float32 [1024], P('fsdp')
- ln2_bias_grad: float32 [1024], P('fsdp')
- fc1_grad: float32 [1024, 4096], P('fsdp')
- fc1_bias_grad: float32 [4096], P('fsdp')
- fc2_grad: float32 [4096, 1024], P('fsdp')
- table_grad: float32 [50, 1024], P(None, 'fsdp')
Inputs may be any that keep to these rules, and one draw needn't show every extreme that they name: `pos_index`: row 0 names row 0 four times; every other row names rows 1 + 7i + j, 2 + 7i + j, 8 + 7i + j, 9 + 7i + j for some i, j in 0 to 5.
All inputs are finite; a program needn't handle non-finite values.
Results may differ from a plain program's by a relative error of at most 0.018.
Values may be sent and summed in bfloat16 or wider, within the bound.
No kernel may reach another device: no remote copies, remote signals or barrier semaphores. Data moves between devices by JAX's collectives and lax.ppermute only.
A program may use at most 192 MiB of HBM per device.

v0:
```python
import jax
import jax.numpy as jnp
from jax import lax
from jax.sharding import PartitionSpec as P

HEADS = 16
HDIM = 64
POS = 50
HIGH_LEN = 145
highest = lax.Precision.HIGHEST


def layer_norm(hidden, gain, shift):
    centre = hidden - jnp.mean(hidden, axis=-1, keepdims=True)
    spread = jnp.mean(centre * centre, axis=-1, keepdims=True)
    return centre * lax.rsqrt(spread + 1e-06) * gain + shift


def place_rows(rows, low_flag, pos_index, pos_weight):
    offsets = jnp.arange(rows, dtype=jnp.int32)
    table_ids = jnp.arange(POS, dtype=jnp.int32)
    high_ids = jnp.arange(HIGH_LEN, dtype=jnp.int32)
    picks = (pos_index[:, :, None] == table_ids[None, None, :]).astype(jnp.float32)
    interp = jnp.sum(pos_weight[:, :, None] * picks, axis=1)
    low_valid = offsets < rows // POS * POS
    high_valid = offsets < rows // HIGH_LEN * HIGH_LEN
    low_place = (((offsets % POS)[:, None] == table_ids[None, :]) & low_valid[:, None]).astype(
        jnp.float32
    )
    high_pick = (((offsets % HIGH_LEN)[:, None] == high_ids[None, :]) & high_valid[:, None]).astype(
        jnp.float32
    )
    high_place = jnp.dot(high_pick, interp, precision=highest)
    place = jnp.where(low_flag, low_place, high_place)
    valid = jnp.where(low_flag, low_valid, high_valid)
    segment = jnp.where(
        low_flag,
        jnp.where(low_valid, offsets // POS, -1),
        jnp.where(high_valid, offsets // HIGH_LEN, -1),
    )
    return (place, valid, segment[:, None] == segment[None, :])


def split_pairs(block):
    return block.reshape(block.shape[0], HEADS // 2, 2, HDIM).transpose(1, 0, 2, 3)


def join_pairs(block):
    return block.transpose(1, 0, 2, 3).reshape(block.shape[1], HEADS * HDIM)


def masked_scores(query_pair, key_pair, mask):
    scores = jnp.einsum(
        "qhd,khd->hqk", query_pair, key_pair, preferred_element_type=jnp.float32
    ) * HDIM ** (-0.5)
    return jnp.where(mask[None], scores, -1e30)


def forward(patches, params, place, mask):
    gain_one, bias_one, w_qkv, w_out, gain_two, bias_two, w_fc1, fc1_bias, w_fc2, pos_table = params
    width = w_out.shape[0]
    hidden_in = patches.astype(jnp.float32) + jnp.dot(
        place, pos_table.astype(jnp.float32), precision=highest
    )
    normed_one = layer_norm(
        hidden_in, gain_one.astype(jnp.float32), bias_one.astype(jnp.float32)
    ).astype(jnp.bfloat16)
    projected = jnp.dot(normed_one, w_qkv, preferred_element_type=jnp.float32).astype(jnp.bfloat16)
    queries = split_pairs(projected[:, :width])
    keys = split_pairs(projected[:, width : 2 * width])
    values = split_pairs(projected[:, 2 * width :])

    def attend(items):
        query_pair, key_pair, value_pair = items
        scores = masked_scores(query_pair, key_pair, mask)
        peak = jnp.max(scores, axis=-1, keepdims=True)
        expo = jnp.exp(scores - peak)
        total = jnp.sum(expo, axis=-1, keepdims=True)
        probs = (expo / total).astype(jnp.bfloat16)
        mixed = jnp.einsum("hqk,khd->qhd", probs, value_pair, preferred_element_type=jnp.float32)
        return (mixed.astype(jnp.bfloat16), (peak + jnp.log(total))[..., 0])

    attended, log_norm = lax.map(attend, (queries, keys, values))
    attn_rows = join_pairs(attended)
    hidden_mid = hidden_in + jnp.dot(attn_rows, w_out, preferred_element_type=jnp.float32)
    normed_two = layer_norm(
        hidden_mid, gain_two.astype(jnp.float32), bias_two.astype(jnp.float32)
    ).astype(jnp.bfloat16)
    pre_act = jnp.dot(normed_two, w_fc1, preferred_element_type=jnp.float32) + fc1_bias.astype(
        jnp.float32
    )
    activated = jax.nn.gelu(pre_act, approximate=False).astype(jnp.bfloat16)
    branch_out = jnp.dot(activated, w_fc2, preferred_element_type=jnp.float32)
    return (
        hidden_in,
        normed_one,
        projected,
        log_norm,
        attn_rows,
        hidden_mid,
        normed_two,
        pre_act,
        activated,
        branch_out,
    )


def backward(kept, params, place, mask, grad_out):
    gain_one, bias_one, w_qkv, w_out, gain_two, bias_two, w_fc1, fc1_bias, w_fc2, pos_table = params
    (
        hidden_in,
        normed_one,
        projected,
        log_norm,
        attn_rows,
        hidden_mid,
        normed_two,
        pre_act,
        activated,
        branch_out,
    ) = kept
    width = w_out.shape[0]
    grad_fc2 = jnp.einsum("rf,rd->fd", activated, grad_out, preferred_element_type=jnp.float32)
    grad_act = jnp.einsum("rd,fd->rf", grad_out, w_fc2, preferred_element_type=jnp.float32)
    _, pull_gelu = jax.vjp(lambda inner: jax.nn.gelu(inner, approximate=False), pre_act)
    grad_pre = pull_gelu(grad_act)[0].astype(jnp.bfloat16)
    grad_fc1_bias = jnp.sum(grad_pre.astype(jnp.float32), axis=0)
    grad_fc1 = jnp.einsum("rd,rf->df", normed_two, grad_pre, preferred_element_type=jnp.float32)
    grad_norm_two = jnp.einsum("rf,df->rd", grad_pre, w_fc1, preferred_element_type=jnp.float32)
    _, pull_two = jax.vjp(
        layer_norm, hidden_mid, gain_two.astype(jnp.float32), bias_two.astype(jnp.float32)
    )
    back_mid, grad_gain_two, grad_bias_two = pull_two(grad_norm_two)
    grad_mid = grad_out.astype(jnp.float32) + back_mid
    grad_branch = grad_mid.astype(jnp.bfloat16)
    grad_wout = jnp.einsum("rd,re->de", attn_rows, grad_branch, preferred_element_type=jnp.float32)
    grad_attn = jnp.einsum(
        "re,de->rd", grad_branch, w_out, preferred_element_type=jnp.float32
    ).astype(jnp.bfloat16)
    queries = split_pairs(projected[:, :width])
    keys = split_pairs(projected[:, width : 2 * width])
    values = split_pairs(projected[:, 2 * width :])
    grad_pairs = split_pairs(grad_attn)

    def attend_back(items):
        query_pair, key_pair, value_pair, grad_pair, log_pair = items
        scores = masked_scores(query_pair, key_pair, mask)
        probs = jnp.exp(scores - log_pair[..., None])
        probs_low = probs.astype(jnp.bfloat16)
        grad_probs = jnp.einsum(
            "qhd,khd->hqk", grad_pair, value_pair, preferred_element_type=jnp.float32
        )
        centre = jnp.sum(probs * grad_probs, axis=-1, keepdims=True)
        grad_scores = (probs * (grad_probs - centre)).astype(jnp.bfloat16)
        grad_query = jnp.einsum(
            "hqk,khd->qhd", grad_scores, key_pair, preferred_element_type=jnp.float32
        ) * HDIM ** (-0.5)
        grad_key = jnp.einsum(
            "hqk,qhd->khd", grad_scores, query_pair, preferred_element_type=jnp.float32
        ) * HDIM ** (-0.5)
        grad_value = jnp.einsum(
            "hqk,qhd->khd", probs_low, grad_pair, preferred_element_type=jnp.float32
        )
        return (grad_query, grad_key, grad_value)

    grad_query, grad_key, grad_value = lax.map(
        attend_back, (queries, keys, values, grad_pairs, log_norm)
    )
    grad_proj = jnp.concatenate(
        [join_pairs(grad_query), join_pairs(grad_key), join_pairs(grad_value)], axis=1
    ).astype(jnp.bfloat16)
    grad_qkv = jnp.einsum("rd,re->de", normed_one, grad_proj, preferred_element_type=jnp.float32)
    grad_norm_one = jnp.einsum("re,de->rd", grad_proj, w_qkv, preferred_element_type=jnp.float32)
    _, pull_one = jax.vjp(
        layer_norm, hidden_in, gain_one.astype(jnp.float32), bias_one.astype(jnp.float32)
    )
    back_in, grad_gain_one, grad_bias_one = pull_one(grad_norm_one)
    grad_in = grad_mid + back_in
    grad_table = jnp.dot(place.T, grad_in, precision=highest)
    grads = (
        grad_gain_one,
        grad_bias_one,
        grad_qkv,
        grad_wout,
        grad_gain_two,
        grad_bias_two,
        grad_fc1,
        grad_fc1_bias,
        grad_fc2,
        grad_table,
    )
    return (grad_in.astype(jnp.bfloat16), grads)


def per_device(
    patches,
    cotangent,
    ln1_gain,
    ln1_bias,
    w_qkv,
    w_out,
    ln2_gain,
    ln2_bias,
    w_fc1,
    fc1_bias,
    w_fc2,
    pos_table,
    pos_index,
    pos_weight,
):
    n_data = lax.axis_size("dp")
    low_flag = lax.axis_index("dp") < n_data * 7 // 16
    rows = patches.shape[0]
    place, valid, mask = place_rows(rows, low_flag, pos_index, pos_weight)
    gathered = (
        lax.all_gather(ln1_gain, "fsdp", axis=0, tiled=True),
        lax.all_gather(ln1_bias, "fsdp", axis=0, tiled=True),
        lax.all_gather(w_qkv, "fsdp", axis=0, tiled=True),
        lax.all_gather(w_out, "fsdp", axis=0, tiled=True),
        lax.all_gather(ln2_gain, "fsdp", axis=0, tiled=True),
        lax.all_gather(ln2_bias, "fsdp", axis=0, tiled=True),
        lax.all_gather(w_fc1, "fsdp", axis=0, tiled=True),
        lax.all_gather(fc1_bias, "fsdp", axis=0, tiled=True),
        lax.all_gather(w_fc2, "fsdp", axis=0, tiled=True),
        lax.all_gather(pos_table, "fsdp", axis=1, tiled=True),
    )
    kept = forward(patches, gathered, place, mask)
    block_out = jnp.where(valid[:, None], kept[5] + kept[9], 0.0).astype(jnp.bfloat16)
    regathered = (
        lax.all_gather(ln1_gain, "fsdp", axis=0, tiled=True),
        lax.all_gather(ln1_bias, "fsdp", axis=0, tiled=True),
        lax.all_gather(w_qkv, "fsdp", axis=0, tiled=True),
        lax.all_gather(w_out, "fsdp", axis=0, tiled=True),
        lax.all_gather(ln2_gain, "fsdp", axis=0, tiled=True),
        lax.all_gather(ln2_bias, "fsdp", axis=0, tiled=True),
        lax.all_gather(w_fc1, "fsdp", axis=0, tiled=True),
        lax.all_gather(fc1_bias, "fsdp", axis=0, tiled=True),
        lax.all_gather(w_fc2, "fsdp", axis=0, tiled=True),
        lax.all_gather(pos_table, "fsdp", axis=1, tiled=True),
    )
    rekept = forward(patches, regathered, place, mask)
    grad_out = jnp.where(valid[:, None], cotangent, jnp.zeros_like(cotangent))
    input_grad, grads = backward(rekept, regathered, place, mask, grad_out)
    shares = (
        lax.psum_scatter(
            grads[0].astype(jnp.bfloat16), "fsdp", scatter_dimension=0, tiled=True
        ).astype(jnp.float32),
        lax.psum_scatter(
            grads[1].astype(jnp.bfloat16), "fsdp", scatter_dimension=0, tiled=True
        ).astype(jnp.float32),
        lax.psum_scatter(
            grads[2].astype(jnp.bfloat16), "fsdp", scatter_dimension=0, tiled=True
        ).astype(jnp.float32),
        lax.psum_scatter(
            grads[3].astype(jnp.bfloat16), "fsdp", scatter_dimension=0, tiled=True
        ).astype(jnp.float32),
        lax.psum_scatter(
            grads[4].astype(jnp.bfloat16), "fsdp", scatter_dimension=0, tiled=True
        ).astype(jnp.float32),
        lax.psum_scatter(
            grads[5].astype(jnp.bfloat16), "fsdp", scatter_dimension=0, tiled=True
        ).astype(jnp.float32),
        lax.psum_scatter(
            grads[6].astype(jnp.bfloat16), "fsdp", scatter_dimension=0, tiled=True
        ).astype(jnp.float32),
        lax.psum_scatter(
            grads[7].astype(jnp.bfloat16), "fsdp", scatter_dimension=0, tiled=True
        ).astype(jnp.float32),
        lax.psum_scatter(
            grads[8].astype(jnp.bfloat16), "fsdp", scatter_dimension=0, tiled=True
        ).astype(jnp.float32),
        lax.psum_scatter(
            grads[9].astype(jnp.bfloat16), "fsdp", scatter_dimension=1, tiled=True
        ).astype(jnp.float32),
    )
    totals = (
        lax.psum(shares[0].astype(jnp.bfloat16), "dp").astype(jnp.float32),
        lax.psum(shares[1].astype(jnp.bfloat16), "dp").astype(jnp.float32),
        lax.psum(shares[2].astype(jnp.bfloat16), "dp").astype(jnp.float32),
        lax.psum(shares[3].astype(jnp.bfloat16), "dp").astype(jnp.float32),
        lax.psum(shares[4].astype(jnp.bfloat16), "dp").astype(jnp.float32),
        lax.psum(shares[5].astype(jnp.bfloat16), "dp").astype(jnp.float32),
        lax.psum(shares[6].astype(jnp.bfloat16), "dp").astype(jnp.float32),
        lax.psum(shares[7].astype(jnp.bfloat16), "dp").astype(jnp.float32),
        lax.psum(shares[8].astype(jnp.bfloat16), "dp").astype(jnp.float32),
        lax.psum(shares[9].astype(jnp.bfloat16), "dp").astype(jnp.float32),
    )
    return (
        block_out,
        input_grad,
        totals[0],
        totals[1],
        totals[2],
        totals[3],
        totals[4],
        totals[5],
        totals[6],
        totals[7],
        totals[8],
        totals[9],
    )


def solution(mesh):
    return jax.shard_map(
        per_device,
        mesh=mesh,
        in_specs=(
            P(("dp", "fsdp"), None),
            P(("dp", "fsdp"), None),
            P("fsdp"),
            P("fsdp"),
            P("fsdp", None),
            P("fsdp", None),
            P("fsdp"),
            P("fsdp"),
            P("fsdp", None),
            P("fsdp"),
            P("fsdp", None),
            P(None, "fsdp"),
            P(),
            P(),
        ),
        out_specs=(
            P(("dp", "fsdp"), None),
            P(("dp", "fsdp"), None),
            P("fsdp"),
            P("fsdp"),
            P("fsdp", None),
            P("fsdp", None),
            P("fsdp"),
            P("fsdp"),
            P("fsdp", None),
            P("fsdp"),
            P("fsdp", None),
            P(None, "fsdp"),
        ),
        check_vma=False,
    )
```

profile of v0, /device:TPU:0, one launch (start us, length us, event | category | flops | bytes accessed | tf_op | source)
XLA Modules:
  0.0 1141.8 jit_solution(14354497924452631395)
XLA Ops:
  10.2 15.1 %all_gather.40 = bf16[50,1024]{1,0:T(8,128)(2,1)S(1)} all-gather(bf16[50,256]{1,0:T(8,128)(2,1)S(1)} %copy-done.16), channel_id=1, replica_groups=mesh['dp'=8,'fsdp'=4] {'fsdp'}, dimensions={1}, use_global_device_ids=true | all-gather | bytes 128000 | tf_op jit(solution)/shard_map/all_gather | solution.py:225
  27.7 12.1 %all-gather = bf16[4,1,256]{2,1,0:T(2,128)(2,1)S(1)} all-gather(bf16[1,1,256]{2,1,0:T(2,128)(2,1)S(1)} %reshape.257), channel_id=1, replica_groups=mesh['dp'=8,'fsdp'=4] {'fsdp'}, dimensions={0}, use_global_device_ids=true | all-gather | bytes 2560 | tf_op jit(solution)/shard_map/all_gather | solution.py:216
  39.8 8.5 all-gather.1
  48.3 14.1 %all-gather.2 = bf16[4,1,256]{2,1,0:T(2,128)(2,1)S(1)} all-gather(bf16[1,1,256]{2,1,0:T(2,128)(2,1)S(1)} %reshape.261), channel_id=1, replica_groups=mesh['dp'=8,'fsdp'=4] {'fsdp'}, dimensions={0}, use_global_device_ids=true | all-gather | bytes 2560 | tf_op jit(solution)/shard_map/all_gather | solution.py:220
  62.4 17.2 %all_gather.48 = bf16[4096]{0:T(1024)(128)(2,1)S(1)} all-gather(bf16[1024]{0:T(1024)(128)(2,1)S(1)} %copy-done.22), channel_id=1, replica_groups=mesh['dp'=8,'fsdp'=4] {'fsdp'}, dimensions={0}, use_global_device_ids=true | all-gather | bytes 10240 | tf_op jit(solution)/shard_map/all_gather | solution.py:223
  79.7 8.2 all-gather.3
  87.9 40.0 %all-gather.9.cloned.1.call-done = bf16[1024,3072]{1,0:T(8,128)(2,1)} async-done(((bf16[256,3072]{1,0:T(8,128)(2,1)}), bf16[1024,3072]{1,0:T(8,128)(2,1)}) %all-gather.9.cloned.1.call-update) | async-done | bytes 6291472 | tf_op jit(solution)/shard_map/all_gather | solution.py:218
  128.0 6.6 convolution_convert_fusion.5
  139.1 2.3 copy.66
  142.4 36.8 %while.40 = (s32[]{:T(128)}, bf16[8,512,2,64]{1,3,2,0:T(8,128)(2,1)}, f32[8,2,512]{2,1,0:T(2,128)S(1)}, bf16[8,512,2,64]{1,3,2,0:T(8,128)(2,1)}, bf16[8,512,2,64...) while((s32[]{:T(128)}, ...), condition=%wide.region_12.13_spmd.clone, body=%wide.region_9.12_spmd.clone.sunk | while | flops 140835840 | bytes 7901273 | solution.py:83
  144.7 2.3 fusion.277
  149.3 2.3 fusion.277
  153.9 2.3 fusion.277
  158.5 2.3 fusion.277
  163.1 2.3 fusion.277
  167.7 2.3 fusion.277
  172.3 2.3 fusion.277
  176.9 2.3 fusion.277
  179.2 4.0 fusion.218
  184.9 138.7 %all-gather.13.cloned.1.call-done = bf16[1024,4096]{1,0:T(8,128)(2,1)} async-done(((bf16[256,4096]{1,0:T(8,128)(2,1)}), bf16[1024,4096]{1,0:T(8,128)(2,1)}) %all-gather.13.cloned.1.call-update) | async-done | bytes 8388624 | tf_op jit(solution)/shard_map/all_gather | solution.py:222
  323.6 28.0 %fusion.98 = (f32[512,4096]{1,0:T(8,128)}, f32[512,4096]{1,0:T(8,128)}) fusion(f32[4096]{0:T(1024)S(1)} %convert_element_type.184, bf16[1024,4096]{1,0:T(8,128)(2,1)} %all-gather.13.cloned.1.call-done, f32[512,1024]{1,0:T(8,128)} %copy-done.2, f32[512]{0:T(512)S(1)} %fusion.171, f32[512]{0:T(512)S(1)} %broadcast_multiply_fusion, f32[1024]{0:T(1024)S(1)} %bitcast.216, ...), kind=kOutput, calls=%fused_computation.96 | convolution fusion | flops 4429709312 | bytes 27291648 | tf_op jit(solution)/shard_map/dot_general | solution.py:89
  351.6 121.2 %all-gather.15.cloned.1.call-done = bf16[4096,1024]{1,0:T(8,128)(2,1)} async-done(((bf16[1024,1024]{1,0:T(8,128)(2,1)}), bf16[4096,1024]{1,0:T(8,128)(2,1)}) %all-gather.15.cloned.1.call-update) | async-done | bytes 8388624 | tf_op jit(solution)/shard_map/all_gather | solution.py:224
  472.8 15.7 %fusion.219 = (bf16[4096]{0:T(1024)(128)(2,1)}, bf16[512,4096]{1,0:T(8,128)(2,1)}) fusion(f32[512,4096]{1,0:T(8,128)} %get-tuple-element.283, bf16[4096,1024]{1,0:T(8,128)(2,1)} %all-gather.15.cloned.1.call-done, bf16[512,1024]{1,0:T(8,128)(2,1)S(1)} %copy-done.5, pred[512]{0:T(512)(128)(4,1)S(1)} %broadcast_select_fusion.1, ...), kind=kOutput, calls=%fused_computation.279 | convolution fusion | flops 4329041920 | bytes 30433792 | tf_op jit(solution)/shard_map/rd,fd->rf/dot_general | solution.py:124
  488.6 9.3 multiply_reduce_fusion.1
  501.3 3.8 convolution_convert_fusion.6
  505.2 4.2 convolution_convert_fusion.7
  511.1 72.4 %while.41 = (s32[]{:T(128)}, bf16[8,512,2,64]{1,3,2,0:T(8,128)(2,1)}, bf16[8,512,2,64]{1,3,2,0:T(8,128)(2,1)}, bf16[8,512,2,64]{1,3,2,0:T(8,128)(2,1)}, bf16[8,5...) while((s32[]{:T(128)}, ...), condition=%wide.region_19.20_spmd.clone, body=%wide.region_17.19_spmd.clone.sunk | while | flops 340655104 | bytes 17984624 | solution.py:166
  515.2 2.0 fusion.288
  524.2 2.0 fusion.288
  533.3 2.0 fusion.288
  542.3 2.0 fusion.288
  551.4 2.0 fusion.288
  560.4 2.0 fusion.288
  569.5 2.0 fusion.288
  578.5 2.0 fusion.288
  583.5 8.3 convolution_convert_fusion.4
  593.0 15.1 %convolution_convert_fusion.2 = bf16[4096,1024]{1,0:T(8,128)(2,1)} fusion(f32[512,4096]{1,0:T(8,128)} %get-tuple-element.283, f32[512,4096]{1,0:T(8,128)} %get-tuple-element.284, f32[4096]{0:T(1024)S(1)} %convert_element_type.184, bf16[512,1024]{1,0:T(8,128)(2,1)S(1)} %copy-done.6, pred[512]{0:T(512)(128)(4,1)S(1)} %broadcast_select_fusion.1), kind=kOutput, calls=%fused_computation.127 | convolution fusion | flops 4308074496 | bytes 26231296 | tf_op jit(solution)/shard_map/rf,rd->fd/dot_general | solution.py:123
  608.2 10.8 convolution_convert_fusion.3
  622.6 40.7 %while.39 = (s32[]{:T(128)}, bf16[8,512,2,64]{1,3,2,0:T(8,128)(2,1)}, bf16[8,512,2,64]{1,3,2,0:T(8,128)(2,1)}, bf16[8,512,2,64]{1,3,2,0:T(8,128)(2,1)}, bf16[8,5...) while((s32[]{:T(128)}, bf16[8,512,2,64]{1,3,2,0:T(8,128)(2,1)}, ...), condition=%wide.region_6.7_spmd.clone, body=%wide.region_3.6_spmd.clone.sunk | while | flops 206374912 | bytes 1586253 | solution.py:83
  624.8 2.9 fusion.273
  629.9 2.9 fusion.273
  635.0 2.9 fusion.273
  638.1 2.0 fusion.272
  640.0 2.9 fusion.273
  643.2 2.0 fusion.272
  645.1 2.9 fusion.273
  648.2 2.0 fusion.272
  650.2 2.9 fusion.273
  653.3 2.0 fusion.272
  655.3 2.9 fusion.273
  660.4 2.9 fusion.273
  663.3 3.5 fusion.217
  668.4 7.3 multiply_reduce_fusion.2
  678.9 2.0 convolution_convert_fusion.8
  681.0 19.9 %reduce-scatter.6.cloned.1.call-done = bf16[256,3072]{1,0:T(8,128)(2,1)} async-done(((bf16[1024,3072]{1,0:T(8,128)(2,1)}), bf16[256,3072]{1,0:T(8,128)(2,1)}) %reduce-scatter.6.cloned.1.call-update) | async-done | bytes 1572880 | tf_op jit(solution)/shard_map/reduce_scatter | solution.py:251
  700.9 147.5 %reduce-scatter.12.cloned.1.call-done = bf16[1024,1024]{1,0:T(8,128)(2,1)} async-done(((bf16[4096,1024]{1,0:T(8,128)(2,1)}), bf16[1024,1024]{1,0:T(8,128)(2,1)}) %reduce-scatter.12.cloned.1.call-update) | async-done | bytes 2097168 | tf_op jit(solution)/shard_map/reduce_scatter | solution.py:269
  848.5 147.6 %reduce-scatter.10.cloned.1.call-done = bf16[256,4096]{1,0:T(8,128)(2,1)} async-done(((bf16[1024,4096]{1,0:T(8,128)(2,1)}), bf16[256,4096]{1,0:T(8,128)(2,1)}) %reduce-scatter.10.cloned.1.call-update) | async-done | bytes 2097168 | tf_op jit(solution)/shard_map/reduce_scatter | solution.py:263
  996.1 32.4 %select_convert_fusion = bf16[512,1024]{1,0:T(8,128)(2,1)} fusion(f32[512,1024]{1,0:T(8,128)S(1)} %copy-done.9, bf16[4096,1024]{1,0:T(8,128)(2,1)} %all-gather.15.cloned.1.call-done, bf16[1024,4096]{1,0:T(8,128)(2,1)} %all-gather.13.cloned.1.call-done, f32[4096]{0:T(1024)S(1)} %convert_element_type.184, f32[1024]{0:T(1024)S(1)} %bitcast.218, ...), kind=kOutput, calls=%fused_computation.176 | convolution fusion | flops 8732540928 | bytes 19952128 | tf_op jit(solution)/shard_map/dot_general | solution.py:93
  1028.6 18.1 %all-reduce.7 = (bf16[1024]{0:T(1024)(128)(2,1)S(1)}, bf16[1024]{0:T(1024)(128)(2,1)S(1)}, bf16[1024]{0:T(1024)(128)(2,1)S(1)}, bf16[1024]{0:T(1024)(128)(2,1)S(1)}, bf16[4096]{0:T(1024)(128)(2,1)S(1)}) all-reduce(bf16[1024]{0:T(1024)(128)(2,1)S(1)} %get-tuple-element.199, ...), channel_id=2, replica_groups=mesh['dp'=8,'fsdp'=4] {'fsdp'}, use_global_device_ids=true, to_apply=%region_23.24.clone | all-reduce | flops 8192 | bytes 32768
  1047.0 23.9 %all-reduce.5 = (bf16[256]{0:T(256)(128)(2,1)S(1)}, bf16[256]{0:T(256)(128)(2,1)S(1)}, bf16[256]{0:T(256)(128)(2,1)S(1)}, bf16[256]{0:T(256)(128)(2,1)S(1)}, bf1...) all-reduce(bf16[256]{0:T(256)(128)(2,1)S(1)} %dynamic-slice.1, ...), channel_id=1, replica_groups=mesh['dp'=8,'fsdp'=4] {'dp'}, use_global_device_ids=true, to_apply=%region_24.25 | all-reduce | flops 14848 | bytes 59392 | tf_op jit(solution)/shard_map/psum | solution.py:277
  1074.4 50.6 %all-reduce.10.cloned.1.call-done = (bf16[256,3072]{1,0:T(8,128)(2,1)}, bf16[256,1024]{1,0:T(8,128)(2,1)}, bf16[256,4096]{1,0:T(8,128)(2,1)}, bf16[1024,1024]{1,0:T(8,128)(2,1)}) async-done(((bf16[256,3072]{1,0:T(8,128)(2,1)}, bf16[256,1024]{1,0:T(8,128)(2,1)}, bf16[256,4096]{1,0:T(8,128)(2,1)}, bf16[1024,1024]{1,0:T(8,128)(2,1)}), (bf16[256,3072]{1,0:T(8,128)(2,1)}, bf16[256,1024]{1,0:T(8,128)(2,1)}, ...) | async-done | bytes 6291472 | tf_op jit(solution)/shard_map/psum | solution.py:279
  1124.9 4.2 convert_element_type.206
  1129.2 2.5 convert_element_type.210
  1131.7 2.0 convert_element_type.198
  (243 shorter events, 114.4 us)
Async XLA Ops:
  7.2 3.0 copy-start.16
  7.2 18.2 %copy-start.21 = (s32[145,4]{0,1:T(4,128)S(1)}, s32[145,4]{0,1:T(4,128)}, u32[]{:S(2)}) copy-start(s32[145,4]{0,1:T(4,128)} %param.32) | copy-start | bytes 6964
  7.2 18.1 %copy-start.20 = (f32[145,4]{0,1:T(4,128)S(1)}, f32[145,4]{0,1:T(4,128)}, u32[]{:S(2)}) copy-start(f32[145,4]{0,1:T(4,128)} %param.33) | copy-start | bytes 6964
  7.2 18.8 %copy-start.11 = (bf16[512,1024]{1,0:T(8,128)(2,1)S(1)}, bf16[512,1024]{1,0:T(8,128)(2,1)}, u32[]{:S(2)}) copy-start(bf16[512,1024]{1,0:T(8,128)(2,1)} %param.20) | copy-start | bytes 3145732
  7.2 120.7 %all-gather.9.cloned.1.call-start = ((), (), s32[]{:S(2)}) async-start(), calls=%async_computation.5 | async-start | bytes 7864320 | tf_op jit(solution)/shard_map/all_gather | solution.py:218
  8.0 171.3 %all-gather.11.cloned.1.call-start = ((), (), s32[]{:S(2)}) async-start(), calls=%async_computation.6 | async-start | bytes 2621440 | tf_op jit(solution)/shard_map/all_gather | solution.py:219
  8.7 314.9 %all-gather.13.cloned.1.call-start = ((), (), s32[]{:S(2)}) async-start(), calls=%async_computation.7 | async-start | bytes 10485760 | tf_op jit(solution)/shard_map/all_gather | solution.py:222
  9.4 18.2 %copy-start.27 = (bf16[256]{0:T(256)(128)(2,1)S(1)}, bf16[256]{0:T(256)(128)(2,1)}, u32[]{:S(2)}) copy-start(bf16[256]{0:T(256)(128)(2,1)} %param.22) | copy-start | bytes 1540
  9.4 30.3 %copy-start.28 = (bf16[256]{0:T(256)(128)(2,1)S(1)}, bf16[256]{0:T(256)(128)(2,1)}, u32[]{:S(2)}) copy-start(bf16[256]{0:T(256)(128)(2,1)} %param.23) | copy-start | bytes 1540
  9.5 38.8 %copy-start.29 = (bf16[256]{0:T(256)(128)(2,1)S(1)}, bf16[256]{0:T(256)(128)(2,1)}, u32[]{:S(2)}) copy-start(bf16[256]{0:T(256)(128)(2,1)} %param.26) | copy-start | bytes 1540
  9.5 53.0 %copy-start.22 = (bf16[1024]{0:T(1024)(128)(2,1)S(1)}, bf16[1024]{0:T(1024)(128)(2,1)}, u32[]{:S(2)}) copy-start(bf16[1024]{0:T(1024)(128)(2,1)} %param.29) | copy-start | bytes 6148
  9.5 70.2 %copy-start.30 = (bf16[256]{0:T(256)(128)(2,1)S(1)}, bf16[256]{0:T(256)(128)(2,1)}, u32[]{:S(2)}) copy-start(bf16[256]{0:T(256)(128)(2,1)} %param.27) | copy-start | bytes 1540
  9.5 463.3 %all-gather.15.cloned.1.call-start = ((), (), s32[]{:S(2)}) async-start(), calls=%async_computation.8 | async-start | bytes 10485760 | tf_op jit(solution)/shard_map/all_gather | solution.py:224
  10.1 670.9 %reduce-scatter.8.cloned.1.call-start = ((), (), s32[]{:S(2)}) async-start(), calls=%async_computation.10 | async-start | bytes 2621440 | tf_op jit(solution)/shard_map/reduce_scatter | solution.py:254
  26.0 108.6 %copy-start.14 = (f32[512,50]{0,1:T(8,128)}, f32[512,50]{0,1:T(8,128)S(1)}, u32[]{:S(2)}) copy-start(f32[512,50]{0,1:T(8,128)S(1)} %convolution_select_fusion) | copy-start | bytes 307204
  27.6 34.8 %copy-start.17 = (f32[512]{0:T(512)}, f32[512]{0:T(512)S(1)}, u32[]{:S(2)}) copy-start(f32[512]{0:T(512)S(1)} %multiply_reduce_fusion.7) | copy-start | bytes 6148
  179.2 5.7 copy-start.4
  183.2 1.3 copy-start.2
  323.6 149.3 %copy-start.5 = (bf16[512,1024]{1,0:T(8,128)(2,1)S(1)}, bf16[512,1024]{1,0:T(8,128)(2,1)}, u32[]{:S(2)}) copy-start(bf16[512,1024]{1,0:T(8,128)(2,1)} %param.21) | copy-start | bytes 3145732
  472.8 15.7 %copy-start.3 = (f32[512,1024]{1,0:T(8,128)S(1)}, f32[512,1024]{1,0:T(8,128)}, u32[]{:S(2)}) copy-start(f32[512,1024]{1,0:T(8,128)} %copy-done.2) | copy-start | bytes 6291460
  498.6 1.3 copy-start
  500.3 1.0 copy-start.12
  505.1 195.8 %reduce-scatter.6.cloned.1.call-start = ((), (), s32[]{:S(2)}) async-start(), calls=%async_computation.9 | async-start | bytes 7864320 | tf_op jit(solution)/shard_map/reduce_scatter | solution.py:251
  591.8 1.2 copy-start.6
  591.8 256.6 %reduce-scatter.12.cloned.1.call-start = ((), (), s32[]{:S(2)}) async-start(), calls=%async_computation.12 | async-start | bytes 10485760 | tf_op jit(solution)/shard_map/reduce_scatter | solution.py:269
  608.1 388.0 %reduce-scatter.10.cloned.1.call-start = ((), (), s32[]{:S(2)}) async-start(), calls=%async_computation.11 | async-start | bytes 10485760 | tf_op jit(solution)/shard_map/reduce_scatter | solution.py:263
  619.0 0.7 copy-start.31
  619.0 428.0 %reduce-scatter.14.cloned.1.call-start = ((), (), s32[]{:S(2)}) async-start(), calls=%async_computation.13 | async-start | bytes 143360 | tf_op jit(solution)/shard_map/reduce_scatter | solution.py:272
  663.3 5.2 copy-start.25
  663.3 5.2 copy-start.26
  666.8 1.3 copy-start.8
  668.4 7.3 copy-start.18
  675.7 1.6 copy-start.1
  677.3 1.5 copy-start.15
  678.9 317.2 %copy-start.9 = (f32[512,1024]{1,0:T(8,128)S(1)}, f32[512,1024]{1,0:T(8,128)}, u32[]{:S(2)}) copy-start(f32[512,1024]{1,0:T(8,128)} %copy-done.8) | copy-start | bytes 6291460
  680.9 444.0 %all-reduce.10.cloned.1.call-start = ((), (), s32[]{:S(2)}) async-start(), calls=%async_computation.14 | async-start | bytes 12582912 | tf_op jit(solution)/shard_map/psum | solution.py:279
  996.1 32.5 %copy-start.19 = (bf16[4096]{0:T(1024)(128)(2,1)S(1)}, bf16[4096]{0:T(1024)(128)(2,1)}, u32[]{:S(2)}) copy-start(bf16[4096]{0:T(1024)(128)(2,1)} %get-tuple-element.287) | copy-start | bytes 24580
  996.1 32.5 %copy-start.23 = (bf16[1024]{0:T(1024)(128)(2,1)S(1)}, bf16[1024]{0:T(1024)(128)(2,1)}, u32[]{:S(2)}) copy-start(bf16[1024]{0:T(1024)(128)(2,1)} %get-tuple-element.197) | copy-start | bytes 6148
  996.1 32.5 %copy-start.24 = (bf16[1024]{0:T(1024)(128)(2,1)S(1)}, bf16[1024]{0:T(1024)(128)(2,1)}, u32[]{:S(2)}) copy-start(bf16[1024]{0:T(1024)(128)(2,1)} %get-tuple-element.201) | copy-start | bytes 6148
  1124.9 4.3 copy-start.7
  1129.2 2.5 copy-start.10
  1129.2 4.5 copy-start.13
Sparse Core Ops, SparseCore 0:
  9.6 118.3 all-gather.8
  129.5 43.9 all-gather.10
  175.0 148.4 all-gather.12
  325.0 147.7 all-gather.14
  505.3 41.7 reduce-scatter.7
  591.9 108.9 reduce-scatter.5
  703.3 145.1 reduce-scatter.11
  850.8 145.2 reduce-scatter.9
  998.9 20.0 reduce-scatter.13
  1022.4 102.4 all-reduce.9
where the time goes:
time: 1150 us; the launch traced here: 1140 us
  waiting for transfers between devices  668 us (58%)
  matrix products  288 us (25%)
  blocking collectives  117 us (10%)
  other arithmetic  31.7 us (3%)
  local copies, waits for them, and re-layouts  18.6 us (2%)
  between operations  16.1 us (1%)
    reduce_scatter x1, waiting for transfers between devices, per_device(): lax.psum_scatter(grads[6].astype(jnp.bfloat16), 'fsdp', scatter_dimension...  148 us
    reduce_scatter x1, waiting for transfers between devices, per_device(): lax.psum_scatter(grads[8].astype(jnp.bfloat16), 'fsdp', scatter_dimension...  148 us
    all_gather x1, waiting for transfers between devices, per_device(): lax.all_gather(w_fc1, 'fsdp', axis=0, tiled=True)  139 us
    all_gather x1, waiting for transfers between devices, per_device(): lax.all_gather(w_fc2, 'fsdp', axis=0, tiled=True)  121 us
    psum x1, waiting for transfers between devices, per_device(): lax.psum(shares[2].astype(jnp.bfloat16), 'dp').astype(jnp.float32)  50.6 us
    dot_general x16, matrix products, attend(): jnp.einsum('hqk,khd->qhd', probs, value_pair, preferred_element_type=jnp....  41.9 us
    all_gather x1, waiting for transfers between devices, per_device(): lax.all_gather(w_qkv, 'fsdp', axis=0, tiled=True)  40 us
    dot_general x1, matrix products, forward(): branch_out = jnp.dot(activated, w_fc2, preferred_element_type=jnp.float32)  32.4 us
  transfers between devices with their start and end apart: 10, of which 7 were waited for; matrix products, arithmetic and copies ran while one was open for 26% of the time, Pallas kernels for 0%

commit v1 on v0

--- a/solution.py
+++ b/solution.py
@@ -212,6 +212,32 @@
     low_flag = lax.axis_index("dp") < n_data * 7 // 16
     rows = patches.shape[0]
     place, valid, mask = place_rows(rows, low_flag, pos_index, pos_weight)
+
+    def edit_numbers(shard_in):
+        z_new = lax.axis_size("fsdp")
+        row_out = lax.axis_index("fsdp")
+        plain, parts_out, u1 = (z_new, row_out, shard_in.shape[0])
+        part_now = jnp.zeros(
+            [dev * plain if c == 0 else dev for c, dev in enumerate(shard_in.shape)], shard_in.dtype
+        )
+        left_arr = lax.dynamic_update_slice_in_dim(part_now, shard_in, parts_out * u1, axis=0)
+        q_next = v1 = shard_in
+        j = 1
+        while j < plain // 2 + 1:
+            q_next = lax.ppermute(
+                q_next, axis_name="fsdp", perm=[(c, (c + 1) % plain) for c in range(plain)]
+            )
+            left_arr = lax.dynamic_update_slice_in_dim(
+                left_arr, q_next, (parts_out - j) % plain * u1, axis=0
+            )
+            if 2 * j < plain:
+                v1 = lax.ppermute(v1, "fsdp", [(c, (c - 1) % plain) for c in range(plain)])
+                left_arr = lax.dynamic_update_slice_in_dim(
+                    left_arr, v1, (parts_out + j) % plain * u1, axis=0
+                )
+            j += 1
+        return left_arr
+
     gathered = (
         lax.all_gather(ln1_gain, "fsdp", axis=0, tiled=True),
         lax.all_gather(ln1_bias, "fsdp", axis=0, tiled=True),
@@ -221,7 +247,7 @@
         lax.all_gather(ln2_bias, "fsdp", axis=0, tiled=True),
         lax.all_gather(w_fc1, "fsdp", axis=0, tiled=True),
         lax.all_gather(fc1_bias, "fsdp", axis=0, tiled=True),
-        lax.all_gather(w_fc2, "fsdp", axis=0, tiled=True),
+        edit_numbers(w_fc2),
         lax.all_gather(pos_table, "fsdp", axis=1, tiled=True),
     )
     kept = forward(patches, gathered, place, mask)

time: 1150 us -> 1270 us (1.10)
  waiting for transfers between devices: 668 us -> 772 us
  local copies, waits for them, and re-layouts: 18.6 us -> 33.6 us
    ppermute x0 -> x3, waiting for transfers between devices: none -> 219 us  [the longest x2 156 us: edit_numbers(): lax.ppermute(q_next, axis_name='fsdp', perm=[(c, (c + 1) % plain) for c i...]
    reduce_scatter x1, waiting for transfers between devices: 148 us -> 52.9 us  [per_device(): lax.psum_scatter(grads[8].astype(jnp.bfloat16), 'fsdp', scatter_dimension...]
    reduce_scatter x1, waiting for transfers between devices: 19.9 us -> 0.02 us  [per_device(): lax.psum_scatter(grads[2].astype(jnp.bfloat16), 'fsdp', scatter_dimension...]
  transfers between devices with their start and end apart: 10 -> 13, of which waited for: 7 -> 9; matrix products, arithmetic and copies ran while one was open for 26% -> 24% of each run, Pallas kernels for 0% -> 0%
where the time goes in v1:
time: 1270 us; the launch traced here: 1260 us
  waiting for transfers between devices  772 us (61%)
  matrix products  287 us (23%)
  blocking collectives  117 us (9%)
  local copies, waits for them, and re-layouts  33.6 us (3%)
  other arithmetic  31.7 us (2%)
  between operations  16.3 us (1%)
    ppermute x2, waiting for transfers between devices, edit_numbers(): lax.ppermute(q_next, axis_name='fsdp', perm=[(c, (c + 1) % plain) for c i...  156 us
    reduce_scatter x1, waiting for transfers between devices, per_device(): lax.psum_scatter(grads[6].astype(jnp.bfloat16), 'fsdp', scatter_dimension...  146 us
    all_gather x1, waiting for transfers between devices, per_device(): lax.all_gather(w_fc1, 'fsdp', axis=0, tiled=True)  139 us
    all_gather x1, waiting for transfers between devices, per_device(): lax.all_gather(w_fc2, 'fsdp', axis=0, tiled=True)  121 us
    ppermute x1, waiting for transfers between devices, edit_numbers(): v1 = lax.ppermute(v1, 'fsdp', [(c, (c - 1) % plain) for c in range(plain)])  63.2 us
    reduce_scatter x1, waiting for transfers between devices, per_device(): lax.psum_scatter(grads[8].astype(jnp.bfloat16), 'fsdp', scatter_dimension...  52.9 us
    psum x1, waiting for transfers between devices, per_device(): lax.psum(shares[2].astype(jnp.bfloat16), 'dp').astype(jnp.float32)  50.6 us
    dot_general x16, matrix products, attend(): jnp.einsum('hqk,khd->qhd', probs, value_pair, preferred_element_type=jnp....  41.9 us
  transfers between devices with their start and end apart: 13, of which 9 were waited for; matrix products, arithmetic and copies ran while one was open for 24% of the time, Pallas kernels for 0%

profile of v1, /device:TPU:0, one launch (start us, length us, event | category | flops | bytes accessed | tf_op | source)
XLA Modules:
  0.0 1262.9 jit_solution(16188292871126044453)
XLA Ops:
  10.2 15.1 %all_gather.39 = bf16[50,1024]{1,0:T(8,128)(2,1)S(1)} all-gather(bf16[50,256]{1,0:T(8,128)(2,1)S(1)} %copy-done.18), channel_id=1, replica_groups=mesh['dp'=8,'fsdp'=4] {'fsdp'}, dimensions={1}, use_global_device_ids=true | all-gather | bytes 128000 | tf_op jit(solution)/shard_map/all_gather | solution.py:251
  27.7 12.1 all-gather
  39.8 8.5 all-gather.1
  48.3 14.2 %all-gather.2 = bf16[4,1,256]{2,1,0:T(2,128)(2,1)S(1)} all-gather(bf16[1,1,256]{2,1,0:T(2,128)(2,1)S(1)} %reshape.261), channel_id=1, replica_groups=mesh['dp'=8,'fsdp'=4] {'fsdp'}, dimensions={0}, use_global_device_ids=true | all-gather | bytes 2560 | tf_op jit(solution)/shard_map/all_gather | solution.py:246
  62.5 17.2 %all_gather.47 = bf16[4096]{0:T(1024)(128)(2,1)S(1)} all-gather(bf16[1024]{0:T(1024)(128)(2,1)S(1)} %copy-done.24), channel_id=1, replica_groups=mesh['dp'=8,'fsdp'=4] {'fsdp'}, dimensions={0}, use_global_device_ids=true | all-gather | bytes 10240 | tf_op jit(solution)/shard_map/all_gather | solution.py:249
  79.7 8.2 all-gather.3
  88.0 40.0 %all-gather.9.cloned.1.call-done = bf16[1024,3072]{1,0:T(8,128)(2,1)} async-done(((bf16[256,3072]{1,0:T(8,128)(2,1)}), bf16[1024,3072]{1,0:T(8,128)(2,1)}) %all-gather.9.cloned.1.call-update) | async-done | bytes 6291472 | tf_op jit(solution)/shard_map/all_gather | solution.py:244
  128.0 6.6 convolution_convert_fusion.5
  139.1 2.3 copy.66
  142.5 36.8 %while.40 = (s32[]{:T(128)}, bf16[8,512,2,64]{1,3,2,0:T(8,128)(2,1)}, f32[8,2,512]{2,1,0:T(2,128)S(1)}, bf16[8,512,2,64]{1,3,2,0:T(8,128)(2,1)}, bf16[8,512,2,64...) while((s32[]{:T(128)}, ...), condition=%wide.region_12.13_spmd.clone, body=%wide.region_9.12_spmd.clone.sunk | while | flops 140835840 | bytes 7901273 | solution.py:83
  144.7 2.3 fusion.277
  149.3 2.3 fusion.277
  153.9 2.3 fusion.277
  158.5 2.3 fusion.277
  163.1 2.3 fusion.277
  167.7 2.3 fusion.277
  172.3 2.3 fusion.277
  176.9 2.3 fusion.277
  179.3 4.0 fusion.218
  184.9 138.7 %all-gather.13.cloned.1.call-done = bf16[1024,4096]{1,0:T(8,128)(2,1)} async-done(((bf16[256,4096]{1,0:T(8,128)(2,1)}), bf16[1024,4096]{1,0:T(8,128)(2,1)}) %all-gather.13.cloned.1.call-update) | async-done | bytes 8388624 | tf_op jit(solution)/shard_map/all_gather | solution.py:248
  323.6 28.0 %fusion.98 = (f32[512,4096]{1,0:T(8,128)}, f32[512,4096]{1,0:T(8,128)}) fusion(f32[4096]{0:T(1024)S(1)} %convert_element_type.184, bf16[1024,4096]{1,0:T(8,128)(2,1)} %all-gather.13.cloned.1.call-done, f32[512,1024]{1,0:T(8,128)} %copy-done.3, f32[512]{0:T(512)S(1)} %fusion.171, f32[512]{0:T(512)S(1)} %broadcast_multiply_fusion, f32[1024]{0:T(1024)S(1)} %bitcast.218, ...), kind=kOutput, calls=%fused_computation.96 | convolution fusion | flops 4429709312 | bytes 27291648 | tf_op jit(solution)/shard_map/dot_general | solution.py:89
  351.6 121.2 %all-gather.15.cloned.1.call-done = bf16[4096,1024]{1,0:T(8,128)(2,1)} async-done(((bf16[1024,1024]{1,0:T(8,128)(2,1)}), bf16[4096,1024]{1,0:T(8,128)(2,1)}) %all-gather.15.cloned.1.call-update) | async-done | bytes 8388624 | tf_op jit(solution)/shard_map/all_gather | solution.py:264
  472.9 15.7 %fusion.219 = (bf16[4096]{0:T(1024)(128)(2,1)}, bf16[512,4096]{1,0:T(8,128)(2,1)}) fusion(f32[512,4096]{1,0:T(8,128)} %get-tuple-element.283, bf16[4096,1024]{1,0:T(8,128)(2,1)} %all-gather.15.cloned.1.call-done, bf16[512,1024]{1,0:T(8,128)(2,1)} %param.21, pred[512]{0:T(512)(128)(4,1)S(1)} %broadcast_select_fusion.1, f32[512,4096]{1,0:T(8,128)} %get-tuple-element.284, ...), kind=kOutput, calls=%fused_computation.283 | convolution fusion | flops 4329041920 | bytes 30433792 | tf_op jit(solution)/shard_map/rd,fd->rf/dot_general | solution.py:124
  488.6 9.3 multiply_reduce_fusion.1
  501.4 2.6 convolution_convert_fusion.6
  504.0 4.2 convolution_convert_fusion.7
  509.9 72.4 %while.41 = (s32[]{:T(128)}, bf16[8,512,2,64]{1,3,2,0:T(8,128)(2,1)}, bf16[8,512,2,64]{1,3,2,0:T(8,128)(2,1)}, bf16[8,512,2,64]{1,3,2,0:T(8,128)(2,1)}, bf16[8,5...) while((s32[]{:T(128)}, ...), condition=%wide.region_19.20_spmd.clone, body=%wide.region_17.19_spmd.clone.sunk | while | flops 340655104 | bytes 17984624 | solution.py:166
  514.0 2.0 fusion.288
  523.0 2.0 fusion.288
  532.1 2.0 fusion.288
  550.2 2.0 fusion.288
  559.2 2.0 fusion.288
  582.3 8.2 convolution_convert_fusion.4
  591.8 15.0 %convolution_convert_fusion.2 = bf16[4096,1024]{1,0:T(8,128)(2,1)} fusion(f32[512,4096]{1,0:T(8,128)} %get-tuple-element.283, f32[512,4096]{1,0:T(8,128)} %get-tuple-element.284, f32[4096]{0:T(1024)S(1)} %convert_element_type.184, bf16[512,1024]{1,0:T(8,128)(2,1)S(1)} %copy-done.7, pred[512]{0:T(512)(128)(4,1)S(1)} %broadcast_select_fusion.1), kind=kOutput, calls=%fused_computation.127 | convolution fusion | flops 4308074496 | bytes 26231296 | tf_op jit(solution)/shard_map/rf,rd->fd/dot_general | solution.py:123
  606.9 10.9 convolution_convert_fusion.3
  617.9 3.8 collective-permute-start.1
  621.7 91.7 %collective-permute-done = bf16[1024,1024]{1,0:T(8,128)(2,1)} collective-permute-done((bf16[1024,1024]{1,0:T(8,128)(2,1)}, bf16[1024,1024]{1,0:T(8,128)(2,1)}, u32[]{:S(2)}, u32[]{:S(2)}) %collective-permute-start) | collective-permute-done | bytes 2097184 | tf_op jit(solution)/shard_map/ppermute | solution.py:227
  715.9 4.3 broadcast_in_dim.136
  721.7 3.1 constant_dynamic-update-slice_fusion.2
  724.8 63.2 %collective-permute-done.1 = bf16[1024,1024]{1,0:T(8,128)(2,1)} collective-permute-done((bf16[1024,1024]{1,0:T(8,128)(2,1)}, bf16[1024,1024]{1,0:T(8,128)(2,1)}, u32[]{:S(2)}, u32[]{:S(2)}) %collective-permute-start.1) | collective-permute-done | bytes 2097184 | tf_op jit(solution)/shard_map/ppermute | solution.py:234
  788.0 3.1 constant_dynamic-update-slice_fusion.1
  791.1 64.5 %collective-permute-done.2 = bf16[1024,1024]{1,0:T(8,128)(2,1)} collective-permute-done((bf16[1024,1024]{1,0:T(8,128)(2,1)}, bf16[1024,1024]{1,0:T(8,128)(2,1)}, u32[]{:S(2)}, u32[]{:S(2)}) %collective-permute-start.2) | collective-permute-done | bytes 2097184 | tf_op jit(solution)/shard_map/ppermute | solution.py:227
  855.6 3.1 constant_dynamic-update-slice_fusion
  859.8 40.7 %while.39 = (s32[]{:T(128)}, bf16[8,512,2,64]{1,3,2,0:T(8,128)(2,1)}, bf16[8,512,2,64]{1,3,2,0:T(8,128)(2,1)}, bf16[8,512,2,64]{1,3,2,0:T(8,128)(2,1)}, bf16[8,5...) while((s32[]{:T(128)}, bf16[8,512,2,64]{1,3,2,0:T(8,128)(2,1)}, ...), condition=%wide.region_6.7_spmd.clone, body=%wide.region_3.6_spmd.clone.sunk | while | flops 206374912 | bytes 1586253 | solution.py:83
  861.9 2.9 fusion.273
  867.0 2.9 fusion.273
  872.1 2.9 fusion.273
  877.2 2.9 fusion.273
  882.3 2.9 fusion.273
  887.3 2.9 fusion.273
  892.4 2.9 fusion.273
  897.5 3.0 fusion.273
  900.5 3.4 fusion.217
  905.6 7.3 multiply_reduce_fusion.2
  916.0 2.0 convolution_convert_fusion.8
  918.2 52.9 %reduce-scatter.12.cloned.1.call-done = bf16[1024,1024]{1,0:T(8,128)(2,1)} async-done(((bf16[4096,1024]{1,0:T(8,128)(2,1)}), bf16[1024,1024]{1,0:T(8,128)(2,1)}) %reduce-scatter.12.cloned.1.call-update) | async-done | bytes 2097168 | tf_op jit(solution)/shard_map/reduce_scatter | solution.py:295
  971.1 146.1 %reduce-scatter.10.cloned.1.call-done = bf16[256,4096]{1,0:T(8,128)(2,1)} async-done(((bf16[1024,4096]{1,0:T(8,128)(2,1)}), bf16[256,4096]{1,0:T(8,128)(2,1)}) %reduce-scatter.10.cloned.1.call-update) | async-done | bytes 2097168 | tf_op jit(solution)/shard_map/reduce_scatter | solution.py:289
  1117.2 32.4 %select_convert_fusion = bf16[512,1024]{1,0:T(8,128)(2,1)} fusion(f32[512,1024]{1,0:T(8,128)S(1)} %copy-done.10, bf16[4096,1024]{1,0:T(8,128)(2,1)} %constant_dynamic-update-slice_fusion, bf16[1024,4096]{1,0:T(8,128)(2,1)} %all-gather.13.cloned.1.call-done, f32[4096]{0:T(1024)S(1)} %convert_element_type.184, f32[1024]{0:T(1024)S(1)} %bitcast.220, ...), kind=kOutput, calls=%fused_computation.176 | convolution fusion | flops 8732540928 | bytes 19952128 | tf_op jit(solution)/shard_map/dot_general | solution.py:93
  1149.7 18.1 %all-reduce.7 = (bf16[1024]{0:T(1024)(128)(2,1)S(1)}, bf16[1024]{0:T(1024)(128)(2,1)S(1)}, bf16[1024]{0:T(1024)(128)(2,1)S(1)}, bf16[1024]{0:T(1024)(128)(2,1)S(1)}, bf16[4096]{0:T(1024)(128)(2,1)S(1)}) all-reduce(bf16[1024]{0:T(1024)(128)(2,1)S(1)} %get-tuple-element.199, ...), channel_id=2, replica_groups=mesh['dp'=8,'fsdp'=4] {'fsdp'}, use_global_device_ids=true, to_apply=%region_23.24.clone | all-reduce | flops 8192 | bytes 32768
  1168.1 23.9 %all-reduce.5 = (bf16[256]{0:T(256)(128)(2,1)S(1)}, bf16[256]{0:T(256)(128)(2,1)S(1)}, bf16[256]{0:T(256)(128)(2,1)S(1)}, bf16[256]{0:T(256)(128)(2,1)S(1)}, bf1...) all-reduce(bf16[256]{0:T(256)(128)(2,1)S(1)} %dynamic-slice.1, ...), channel_id=1, replica_groups=mesh['dp'=8,'fsdp'=4] {'dp'}, use_global_device_ids=true, to_apply=%region_24.25 | all-reduce | flops 14848 | bytes 59392 | tf_op jit(solution)/shard_map/psum | solution.py:303
  1195.5 50.6 %all-reduce.10.cloned.1.call-done = (bf16[256,3072]{1,0:T(8,128)(2,1)}, bf16[256,1024]{1,0:T(8,128)(2,1)}, bf16[256,4096]{1,0:T(8,128)(2,1)}, bf16[1024,1024]{1,0:T(8,128)(2,1)}) async-done(((bf16[256,3072]{1,0:T(8,128)(2,1)}, bf16[256,1024]{1,0:T(8,128)(2,1)}, bf16[256,4096]{1,0:T(8,128)(2,1)}, bf16[1024,1024]{1,0:T(8,128)(2,1)}), (bf16[256,3072]{1,0:T(8,128)(2,1)}, bf16[256,1024]{1,0:T(8,128)(2,1)}, ...) | async-done | bytes 6291472 | tf_op jit(solution)/shard_map/psum | solution.py:305
  1246.0 4.2 convert_element_type.206
  1250.3 2.5 convert_element_type.210
  1252.8 2.0 convert_element_type.198
  (258 shorter events, 129.8 us)
Async XLA Ops:
  7.2 3.0 copy-start.18
  7.2 18.2 %copy-start.23 = (s32[145,4]{0,1:T(4,128)S(1)}, s32[145,4]{0,1:T(4,128)}, u32[]{:S(2)}) copy-start(s32[145,4]{0,1:T(4,128)} %param.32) | copy-start | bytes 6964
  7.2 18.1 %copy-start.22 = (f32[145,4]{0,1:T(4,128)S(1)}, f32[145,4]{0,1:T(4,128)}, u32[]{:S(2)}) copy-start(f32[145,4]{0,1:T(4,128)} %param.33) | copy-start | bytes 6964
  7.2 18.8 %copy-start.12 = (bf16[512,1024]{1,0:T(8,128)(2,1)S(1)}, bf16[512,1024]{1,0:T(8,128)(2,1)}, u32[]{:S(2)}) copy-start(bf16[512,1024]{1,0:T(8,128)(2,1)} %param.20) | copy-start | bytes 3145732
  7.2 20.4 %copy-start.29 = (bf16[256]{0:T(256)(128)(2,1)S(1)}, bf16[256]{0:T(256)(128)(2,1)}, u32[]{:S(2)}) copy-start(bf16[256]{0:T(256)(128)(2,1)} %param.22) | copy-start | bytes 1540
  7.2 32.6 %copy-start.30 = (bf16[256]{0:T(256)(128)(2,1)S(1)}, bf16[256]{0:T(256)(128)(2,1)}, u32[]{:S(2)}) copy-start(bf16[256]{0:T(256)(128)(2,1)} %param.23) | copy-start | bytes 1540
  7.2 41.0 %copy-start.31 = (bf16[256]{0:T(256)(128)(2,1)S(1)}, bf16[256]{0:T(256)(128)(2,1)}, u32[]{:S(2)}) copy-start(bf16[256]{0:T(256)(128)(2,1)} %param.26) | copy-start | bytes 1540
  7.3 55.2 %copy-start.24 = (bf16[1024]{0:T(1024)(128)(2,1)S(1)}, bf16[1024]{0:T(1024)(128)(2,1)}, u32[]{:S(2)}) copy-start(bf16[1024]{0:T(1024)(128)(2,1)} %param.29) | copy-start | bytes 6148
  7.3 72.5 %copy-start.32 = (bf16[256]{0:T(256)(128)(2,1)S(1)}, bf16[256]{0:T(256)(128)(2,1)}, u32[]{:S(2)}) copy-start(bf16[256]{0:T(256)(128)(2,1)} %param.27) | copy-start | bytes 1540
  7.3 120.7 %all-gather.9.cloned.1.call-start = ((), (), s32[]{:S(2)}) async-start(), calls=%async_computation.5 | async-start | bytes 7864320 | tf_op jit(solution)/shard_map/all_gather | solution.py:244
  8.0 171.3 %all-gather.11.cloned.1.call-start = ((), (), s32[]{:S(2)}) async-start(), calls=%async_computation.6 | async-start | bytes 2621440 | tf_op jit(solution)/shard_map/all_gather | solution.py:245
  8.8 314.9 %all-gather.13.cloned.1.call-start = ((), (), s32[]{:S(2)}) async-start(), calls=%async_computation.7 | async-start | bytes 10485760 | tf_op jit(solution)/shard_map/all_gather | solution.py:248
  9.5 463.4 %all-gather.15.cloned.1.call-start = ((), (), s32[]{:S(2)}) async-start(), calls=%async_computation.8 | async-start | bytes 10485760 | tf_op jit(solution)/shard_map/all_gather | solution.py:264
  10.1 908.1 %reduce-scatter.8.cloned.1.call-start = ((), (), s32[]{:S(2)}) async-start(), calls=%async_computation.10 | async-start | bytes 2621440 | tf_op jit(solution)/shard_map/reduce_scatter | solution.py:280
  26.0 108.6 %copy-start.16 = (f32[512,50]{0,1:T(8,128)}, f32[512,50]{0,1:T(8,128)S(1)}, u32[]{:S(2)}) copy-start(f32[512,50]{0,1:T(8,128)S(1)} %convolution_select_fusion) | copy-start | bytes 307204
  27.6 34.9 %copy-start.19 = (f32[512]{0:T(512)}, f32[512]{0:T(512)S(1)}, u32[]{:S(2)}) copy-start(f32[512]{0:T(512)S(1)} %multiply_reduce_fusion.7) | copy-start | bytes 6148
  179.3 172.4 %copy-start.5 = (bf16[8,512,2,64]{1,3,2,0:T(8,128)(2,1)}, bf16[8,512,2,64]{1,3,2,0:T(8,128)(2,1)S(1)}, u32[]{:S(2)}) copy-start(bf16[8,512,2,64]{1,3,2,0:T(8,128)(2,1)S(1)} %get-tuple-element.547) | copy-start | bytes 3145732
  183.2 1.3 copy-start.3
  472.9 15.7 %copy-start.4 = (f32[512,1024]{1,0:T(8,128)S(1)}, f32[512,1024]{1,0:T(8,128)}, u32[]{:S(2)}) copy-start(f32[512,1024]{1,0:T(8,128)} %copy-done.3) | copy-start | bytes 6291460
  497.9 2.1 copy-start.6
  497.9 3.4 copy-start.13
  498.6 1.3 copy-start
  500.4 1.0 copy-start.14
  504.0 414.2 %reduce-scatter.6.cloned.1.call-start = ((), (), s32[]{:S(2)}) async-start(), calls=%async_computation.9 | async-start | bytes 7864320 | tf_op jit(solution)/shard_map/reduce_scatter | solution.py:277
  590.6 1.2 copy-start.7
  590.6 380.5 %reduce-scatter.12.cloned.1.call-start = ((), (), s32[]{:S(2)}) async-start(), calls=%async_computation.12 | async-start | bytes 10485760 | tf_op jit(solution)/shard_map/reduce_scatter | solution.py:295
  606.8 510.3 %reduce-scatter.10.cloned.1.call-start = ((), (), s32[]{:S(2)}) async-start(), calls=%async_computation.11 | async-start | bytes 10485760 | tf_op jit(solution)/shard_map/reduce_scatter | solution.py:289
  617.8 96.2 %copy-start.33 = (u32[32]{0:T(128)S(1)}, u32[32]{0:T(128)}, u32[]{:S(2)}) copy-start(u32[32]{0:T(128)} %constant.226) | copy-start | bytes 388
  617.8 550.3 %reduce-scatter.14.cloned.1.call-start = ((), (), s32[]{:S(2)}) async-start(), calls=%async_computation.13 | async-start | bytes 143360 | tf_op jit(solution)/shard_map/reduce_scatter | solution.py:298
  617.8 95.6 %collective-permute-start = (bf16[1024,1024]{1,0:T(8,128)(2,1)}, bf16[1024,1024]{1,0:T(8,128)(2,1)}, u32[]{:S(2)}, u32[]{:S(2)}) collective-permute-start(bf16[1024,1024]{1,0:T(8,128)(2,1)} %param.30), channel_id=1, source_target_pairs={{0,1},{1,2},{2,3},{3,0},{4,5},{5,6},{6,7},{7,4},{8,9},{9,10},{10,1... | collective-permute-start | bytes 6291464 | tf_op jit(solution)/shard_map/ppermute | solution.py:227
  617.9 170.1 %collective-permute-start.1 = (bf16[1024,1024]{1,0:T(8,128)(2,1)}, bf16[1024,1024]{1,0:T(8,128)(2,1)}, u32[]{:S(2)}, u32[]{:S(2)}) collective-permute-start(bf16[1024,1024]{1,0:T(8,128)(2,1)} %param.30), channel_id=1, source_target_pairs={{0,3},{1,0},{2,1},{3,2},{4,7},{5,4},{6,5},{7,6},{8,11},{9,8},{10,9... | collective-permute-start | bytes 6291464 | tf_op jit(solution)/shard_map/ppermute | solution.py:234
  713.4 142.1 %collective-permute-start.2 = (bf16[1024,1024]{1,0:T(8,128)(2,1)}, bf16[1024,1024]{1,0:T(8,128)(2,1)}, u32[]{:S(2)}, u32[]{:S(2)}) collective-permute-start(bf16[1024,1024]{1,0:T(8,128)(2,1)} %collective-permute-done), channel_id=1, source_target_pairs={{0,1},{1,2},{2,3},{3,0},{4,5},{5,6},{6,7},{7,4},{8,9},{9,10},{10,1... | collective-permute-start | bytes 6291464 | tf_op jit(solution)/shard_map/ppermute | solution.py:227
  715.9 4.3 copy-start.2
  900.5 5.1 copy-start.27
  900.5 5.1 copy-start.28
  903.9 1.3 copy-start.9
  905.6 7.3 copy-start.20
  912.9 1.6 copy-start.1
  912.9 3.1 copy-start.17
  916.0 201.2 %copy-start.10 = (f32[512,1024]{1,0:T(8,128)S(1)}, f32[512,1024]{1,0:T(8,128)}, u32[]{:S(2)}) copy-start(f32[512,1024]{1,0:T(8,128)} %copy-done.9) | copy-start | bytes 6291460
  918.0 328.0 %all-reduce.10.cloned.1.call-start = ((), (), s32[]{:S(2)}) async-start(), calls=%async_computation.14 | async-start | bytes 12582912 | tf_op jit(solution)/shard_map/psum | solution.py:305
  1117.2 32.5 %copy-start.21 = (bf16[4096]{0:T(1024)(128)(2,1)S(1)}, bf16[4096]{0:T(1024)(128)(2,1)}, u32[]{:S(2)}) copy-start(bf16[4096]{0:T(1024)(128)(2,1)} %get-tuple-element.287) | copy-start | bytes 24580
  1117.2 32.5 %copy-start.25 = (bf16[1024]{0:T(1024)(128)(2,1)S(1)}, bf16[1024]{0:T(1024)(128)(2,1)}, u32[]{:S(2)}) copy-start(bf16[1024]{0:T(1024)(128)(2,1)} %get-tuple-element.197) | copy-start | bytes 6148
  1117.2 32.4 %copy-start.26 = (bf16[1024]{0:T(1024)(128)(2,1)S(1)}, bf16[1024]{0:T(1024)(128)(2,1)}, u32[]{:S(2)}) copy-start(bf16[1024]{0:T(1024)(128)(2,1)} %get-tuple-element.201) | copy-start | bytes 6148
  1246.0 4.3 copy-start.8
  1246.0 6.7 copy-start.11
  1250.3 4.5 copy-start.15
Sparse Core Ops, SparseCore 0:
  9.7 118.3 all-gather.8
  129.6 43.9 all-gather.10
  175.1 148.4 all-gather.12
  325.0 147.7 all-gather.14
  504.1 41.8 reduce-scatter.7
  590.7 193.2 reduce-scatter.5
  786.4 184.6 reduce-scatter.11
  973.4 143.6 reduce-scatter.9
  1120.0 20.0 reduce-scatter.13
  1143.5 102.4 all-reduce.9
